TPU v7x, 32 devices: a whole 2x2x4 slice. The times are simulated.
32 devices in a mesh: dev: 8 (over z, x), ma: 4 (over y, core).
Axes of the slice: x: 2, y: 2, z: 4, core: 2. Of those that a mesh axis runs over, the one named last changes fastest.
Arguments:
- inputs: bfloat16 [8192, 2048], P('ma', 'dev'), may hold values from -6 to 6
- cotangent: bfloat16 [8192, 2048], P('ma', 'dev'), may hold values from -6 to 6
- factors: bfloat16 [4, 64, 16384], P(None, 'ma', 'dev'), may hold values from -0.5 to 0.5
- exponents: int32 [4, 64], P(None, 'ma'), may hold values from -6 to -4
- error_buffer: bfloat16 [8, 4, 64, 16384], P('dev', None, 'ma'), may hold values from -96 to 96
Outputs:
- output: bfloat16 [8192, 2048], P('ma', 'dev')
- input_grad: bfloat16 [8192, 2048], P('ma', 'dev')
- grad_mean: float32 [4, 64, 16384], P(None, 'ma', 'dev')
- new_error: bfloat16 [8, 4, 64, 16384], P('dev', None, 'ma')
All inputs are finite; a program needn't handle non-finite values.
Results may differ from a plain program's by a relative error of at most 0.0057.
Values may be sent and summed in bfloat16 or wider, within the bound.
A program may use at most 64 MiB of HBM per device.

v0:
```python
import jax
import jax.numpy as jnp
from jax import lax
from jax.sharding import PartitionSpec as P

B = 128


code_limit = 127.0


def regroup(stacked):
    groups = lax.axis_size("ma")
    count, local_blocks, width, tok_count = stacked.shape
    folded = stacked.reshape(
        count, local_blocks, width // (groups * local_blocks), groups, local_blocks, tok_count
    )
    shaped = jnp.transpose(folded, (0, 4, 2, 3, 1, 5))
    arrived = lax.all_to_all(shaped, "ma", split_axis=3, concat_axis=3, tiled=True)
    return arrived.reshape(count, local_blocks, width, tok_count)


def block_forward(weights, values):
    return jnp.einsum("ncd,nct->ndt", weights, values, preferred_element_type=jnp.float32)


def block_backward(weights, values):
    return jnp.einsum("ncd,ndt->nct", weights, values, preferred_element_type=jnp.float32)


def outer_sum(left, right):
    return jnp.einsum("nct,ndt->ncd", left, right, preferred_element_type=jnp.float32)


def quantize(gradients, error_part, exponent_part):
    totals = gradients.reshape(gradients.shape[:-2] + (-1,)) + error_part.astype(jnp.float32)
    scale_inverse = jnp.left_shift(jnp.ones_like(exponent_part), -exponent_part).astype(
        jnp.float32
    )[..., None]
    code_values = jnp.clip(totals * scale_inverse, -code_limit, code_limit)
    return (code_values, (totals - code_values / scale_inverse).astype(jnp.bfloat16), scale_inverse)


def body(inputs, cotangent, factors, exponents, error_buffer):
    local_blocks = factors.shape[1]
    tok_count = inputs.shape[1]
    group_count = lax.axis_size("dev")
    gathered = lax.all_gather(factors, "dev", axis=2, tiled=True)
    matrices = gathered.reshape(gathered.shape[0], local_blocks, B, B)
    block_in = inputs.reshape(local_blocks, B, tok_count)
    block_cot = cotangent.reshape(local_blocks, B, tok_count)
    first_out = block_forward(matrices[0], block_in).astype(jnp.bfloat16)
    mixed_one = regroup(first_out[None])[0]
    second_out = block_forward(matrices[1], mixed_one).astype(jnp.bfloat16)
    pre_gelu = regroup(second_out[None])[0]
    hidden_wide, gelu_back = jax.vjp(jax.nn.gelu, pre_gelu.astype(jnp.float32))
    hidden = hidden_wide.astype(jnp.bfloat16)
    third_out = block_forward(matrices[2], hidden).astype(jnp.bfloat16)
    mixed_two = regroup(third_out[None])[0]
    fourth_out = block_forward(matrices[3], mixed_two).astype(jnp.bfloat16)
    returned = regroup(fourth_out[None])[0]
    output = (block_in.astype(jnp.float32) + returned.astype(jnp.float32)).astype(jnp.bfloat16)
    back_four = regroup(block_cot[None])[0]
    d_mixed_two = block_backward(matrices[3], back_four).astype(jnp.bfloat16)
    gradient_three = outer_sum(mixed_two, back_four)
    d_third = regroup(d_mixed_two[None])[0]
    d_pre = gelu_back(block_backward(matrices[2], d_third))[0].astype(jnp.bfloat16)
    gradient_two = outer_sum(hidden, d_third)
    d_second = regroup(d_pre[None])[0]
    d_mixed_one = block_backward(matrices[1], d_second).astype(jnp.bfloat16)
    gradient_one = outer_sum(mixed_one, d_second)
    d_first = regroup(d_mixed_one[None])[0]
    input_grad = (block_cot.astype(jnp.float32) + block_backward(matrices[0], d_first)).astype(
        jnp.bfloat16
    )
    gradient_zero = outer_sum(block_in, d_first)
    gradients = jnp.stack([gradient_zero, gradient_one, gradient_two, gradient_three])
    code_values, new_part, scale_inverse = quantize(gradients, error_buffer[0], exponents)
    summed = lax.psum_scatter(code_values, "dev", scatter_dimension=2, tiled=True)
    grad_mean = summed / scale_inverse / group_count
    new_error = new_part[None]
    return (
        output.reshape(local_blocks * B, tok_count),
        input_grad.reshape(local_blocks * B, tok_count),
        grad_mean,
        new_error,
    )


def solution(mesh):
    in_specs = (
        P("ma", "dev"),
        P("ma", "dev"),
        P(None, "ma", "dev"),
        P(None, "ma"),
        P("dev", None, "ma", None),
    )
    out_specs = (P("ma", "dev"), P("ma", "dev"), P(None, "ma", "dev"), P("dev", None, "ma", None))
    return jax.shard_map(body, mesh=mesh, in_specs=in_specs, out_specs=out_specs, check_vma=False)
```

profile of v0, /device:TPU:25, one launch (start us, length us, event | category | flops | bytes accessed | tf_op | source)
XLA Modules:
  0.0 290.4 jit_solution(14815720484470332092)
XLA Ops:
  7.9 2.8 copy.67
  10.7 4.2 %all-to-all-start.4 = ((bf16[1,16,2,4,16,256]{5,4,2,1,0,3:T(8,128)(2,1)}), bf16[1,16,2,4,16,256]{5,4,2,1,0,3:T(8,128)(2,1)S(1)}, u32[]{:S(2)}, u32[]{:S(2)}) async-start(bf16[1,16,2,4,16,256]{5,4,2,1,0,3:T(8,128)(2,1)} %copy.67), calls=%async_computation.4 | async-start | bytes 2097152 | tf_op jit(solution)/shard_map/all_to_all | solution.py:19
  14.8 43.4 %all-gather.2.cloned.1.call-done = bf16[4,16,16384]{2,1,0:T(8,128)(2,1)} async-done(((bf16[4,16,2048]{2,1,0:T(8,128)(2,1)}), bf16[4,16,16384]{2,1,0:T(8,128)(2,1)}) %all-gather.2.cloned.1.call-update) | async-done | bytes 2097168 | tf_op jit(solution)/shard_map/all_gather | solution.py:48
  58.2 2.7 slice_bitcast_fusion
  63.4 5.4 %all-to-all-start = ((bf16[1,16,2,4,16,256]{5,1,2,4,0,3:T(8,128)(2,1)}), bf16[1,16,2,4,16,256]{5,1,2,4,0,3:T(8,128)(2,1)}, u32[]{:S(2)}, u32[]{:S(2)}) async-start(bf16[1,16,2,4,16,256]{5,1,2,4,0,3:T(8,128)(2,1)} %bitcast.115), calls=%async_computation | async-start | bytes 2097152 | tf_op jit(solution)/shard_map/all_to_all | solution.py:19
  72.3 10.1 %all-to-all-done = bf16[1,16,2,4,16,256]{5,1,2,4,0,3:T(8,128)(2,1)} async-done(((bf16[1,16,2,4,16,256]{5,1,2,4,0,3:T(8,128)(2,1)}), bf16[1,16,2,4,16,256]{5,1,2,4,0,3:T(8,128)(2,1)}, u32[]{:S(2)}, u32[]{:S(2)}) %all-to-all-start) | async-done | bytes 1048608 | tf_op jit(solution)/shard_map/all_to_all | solution.py:19
  82.4 5.2 %all-to-all-start.5 = ((bf16[1,16,2,4,16,256]{5,1,2,4,0,3:T(8,128)(2,1)}), bf16[1,16,2,4,16,256]{5,1,2,4,0,3:T(8,128)(2,1)}, u32[]{:S(2)}, u32[]{:S(2)}) async-start(bf16[1,16,2,4,16,256]{5,1,2,4,0,3:T(8,128)(2,1)} %bitcast.111), calls=%async_computation.5 | async-start | bytes 2097152 | tf_op jit(solution)/shard_map/all_to_all | solution.py:19
  87.7 2.0 copy.57
  91.3 9.9 %all-to-all-done.5 = bf16[1,16,2,4,16,256]{5,1,2,4,0,3:T(8,128)(2,1)} async-done(((bf16[1,16,2,4,16,256]{5,1,2,4,0,3:T(8,128)(2,1)}), bf16[1,16,2,4,16,256]{5,1,2,4,0,3:T(8,128)(2,1)}, u32[]{:S(2)}, u32[]{:S(2)}) %all-to-all-start.5) | async-done | bytes 1048608 | tf_op jit(solution)/shard_map/all_to_all | solution.py:19
  101.2 5.2 %all-to-all-start.1 = ((bf16[1,16,2,4,16,256]{5,1,2,4,0,3:T(8,128)(2,1)}), bf16[1,16,2,4,16,256]{5,1,2,4,0,3:T(8,128)(2,1)}, u32[]{:S(2)}, u32[]{:S(2)}) async-start(bf16[1,16,2,4,16,256]{5,1,2,4,0,3:T(8,128)(2,1)} %bitcast.138), calls=%async_computation.1 | async-start | bytes 2097152 | tf_op jit(solution)/shard_map/all_to_all | solution.py:19
  106.3 1.9 copy.83
  108.3 2.8 copy.70
  111.0 8.9 %all-to-all-done.1 = bf16[1,16,2,4,16,256]{5,1,2,4,0,3:T(8,128)(2,1)} async-done(((bf16[1,16,2,4,16,256]{5,1,2,4,0,3:T(8,128)(2,1)}), bf16[1,16,2,4,16,256]{5,1,2,4,0,3:T(8,128)(2,1)}, u32[]{:S(2)}, u32[]{:S(2)}) %all-to-all-start.1) | async-done | bytes 1048608 | tf_op jit(solution)/shard_map/all_to_all | solution.py:19
  119.9 2.0 copy.60
  121.9 1.6 fusion.9
  124.6 5.2 %all-to-all-start.6 = ((bf16[1,16,2,4,16,256]{5,1,2,4,0,3:T(8,128)(2,1)}), bf16[1,16,2,4,16,256]{5,1,2,4,0,3:T(8,128)(2,1)}, u32[]{:S(2)}, u32[]{:S(2)}) async-start(bf16[1,16,2,4,16,256]{5,1,2,4,0,3:T(8,128)(2,1)} %bitcast.140), calls=%async_computation.6 | async-start | bytes 2097152 | tf_op jit(solution)/shard_map/all_to_all | solution.py:19
  129.8 2.6 convolution_convert_fusion.3
  133.5 9.8 %all-to-all-done.6 = bf16[1,16,2,4,16,256]{5,1,2,4,0,3:T(8,128)(2,1)} async-done(((bf16[1,16,2,4,16,256]{5,1,2,4,0,3:T(8,128)(2,1)}), bf16[1,16,2,4,16,256]{5,1,2,4,0,3:T(8,128)(2,1)}, u32[]{:S(2)}, u32[]{:S(2)}) %all-to-all-start.6) | async-done | bytes 1048608 | tf_op jit(solution)/shard_map/all_to_all | solution.py:19
  143.3 5.2 %all-to-all-start.2 = ((bf16[1,16,2,4,16,256]{5,1,2,4,0,3:T(8,128)(2,1)}), bf16[1,16,2,4,16,256]{5,1,2,4,0,3:T(8,128)(2,1)}, u32[]{:S(2)}, u32[]{:S(2)}) async-start(bf16[1,16,2,4,16,256]{5,1,2,4,0,3:T(8,128)(2,1)} %bitcast.137), calls=%async_computation.2 | async-start | bytes 2097152 | tf_op jit(solution)/shard_map/all_to_all | solution.py:19
  148.5 1.9 copy.72
  151.8 1.1 copy.92
  152.9 9.1 %all-to-all-done.2 = bf16[1,16,2,4,16,256]{5,1,2,4,0,3:T(8,128)(2,1)} async-done(((bf16[1,16,2,4,16,256]{5,1,2,4,0,3:T(8,128)(2,1)}), bf16[1,16,2,4,16,256]{5,1,2,4,0,3:T(8,128)(2,1)}, u32[]{:S(2)}, u32[]{:S(2)}) %all-to-all-start.2) | async-done | bytes 1048608 | tf_op jit(solution)/shard_map/all_to_all | solution.py:19
  162.1 5.2 %all-to-all-start.7 = ((bf16[1,16,2,4,16,256]{5,1,2,4,0,3:T(8,128)(2,1)}), bf16[1,16,2,4,16,256]{5,1,2,4,0,3:T(8,128)(2,1)}, u32[]{:S(2)}, u32[]{:S(2)}) async-start(bf16[1,16,2,4,16,256]{5,1,2,4,0,3:T(8,128)(2,1)} %bitcast.136), calls=%async_computation.7 | async-start | bytes 2097152 | tf_op jit(solution)/shard_map/all_to_all | solution.py:19
  167.3 3.6 %fusion.15 = f32[16,128,128]{2,1,0:T(8,128)} fusion(bf16[16,128,256]{2,1,0:T(8,128)(2,1)} %bitcast.150, f32[16,128,256]{2,1,0:T(8,128)} %bitcast.148), kind=kOutput, calls=%fused_computation.45 | convolution fusion | flops 138936320 | bytes 4194304 | tf_op jit(solution)/shard_map/nct,ndt->ncd/dot_general | solution.py:32
  170.9 2.4 stack.27
  173.3 2.6 fusion.16
  175.9 2.4 stack.26
  178.3 1.8 copy.63
  181.6 1.3 stack.28
  182.9 1.8 copy.74
  184.7 1.5 convolution_bitcast_fusion
  186.2 1.6 copy.75
  187.8 1.4 stack.25
  189.1 5.4 %fusion.2 = f32[4,16,16384]{2,1,0:T(8,128)} fusion(bf16[1,4,16,16384]{3,2,1,0:T(8,128)(2,1)} %param.9, f32[1,16,16384]{2,1,0:T(8,128)} %stack.28, f32[1,16,16384]{2,1,0:T(8,128)} %stack.27, f32[1,16,16384]{2,1,0:T(8,128)} %stack.26, f32[1,16,16384]{2,1,0:T(8,128)} %stack.25, f32[4,16]{1,0:T(4,128)S(1)} %shift-left_convert_fusion), kind=kLoop, calls=%fused_computation.4 | loop fusion | flops 7340032 | bytes 10486016 | tf_op jit(solution)/shard_map/jit(clip)/min | solution.py:40
  194.5 1.2 copy-done.4
  195.7 1.5 convolution_convert_fusion.2
  198.4 4.6 %all-to-all-start.3 = ((bf16[1,16,2,4,16,256]{5,1,2,4,0,3:T(8,128)(2,1)}), bf16[1,16,2,4,16,256]{5,1,2,4,0,3:T(8,128)(2,1)}, u32[]{:S(2)}, u32[]{:S(2)}) async-start(bf16[1,16,2,4,16,256]{5,1,2,4,0,3:T(8,128)(2,1)} %bitcast.139), calls=%async_computation.3 | async-start | bytes 2097152 | tf_op jit(solution)/shard_map/all_to_all | solution.py:19
  203.0 2.4 stack.32
  205.4 1.2 stack.31
  206.6 2.5 stack.33
  209.0 1.2 stack.30
  210.2 6.3 %all-to-all-done.3 = bf16[1,16,2,4,16,256]{5,1,2,4,0,3:T(8,128)(2,1)} async-done(((bf16[1,16,2,4,16,256]{5,1,2,4,0,3:T(8,128)(2,1)}), bf16[1,16,2,4,16,256]{5,1,2,4,0,3:T(8,128)(2,1)}, u32[]{:S(2)}, u32[]{:S(2)}) %all-to-all-start.3) | async-done | bytes 1048608 | tf_op jit(solution)/shard_map/all_to_all | solution.py:19
  216.6 1.9 copy.66
  218.5 1.4 fusion.10
  220.0 1.3 fusion.11
  222.4 1.9 subtract_convert_fusion
  224.4 57.3 %reduce-scatter.2.cloned.1.call-done = f32[4,16,2048]{2,1,0:T(8,128)} async-done(((f32[4,16,16384]{2,1,0:T(8,128)}), f32[4,16,2048]{2,1,0:T(8,128)}) %reduce-scatter.2.cloned.1.call-update) | async-done | bytes 524304 | tf_op jit(solution)/shard_map/reduce_scatter | solution.py:79
  281.6 1.9 divide_multiply_fusion
  (71 shorter events, 15.7 us)
Async XLA Ops:
  7.2 51.0 %all-gather.2.cloned.1.call-start = ((), (), s32[]{:S(2)}) async-start(), calls=%async_computation.9 | async-start | bytes 2359296 | tf_op jit(solution)/shard_map/all_gather | solution.py:48
  10.7 52.7 %all-to-all-start.4 = ((bf16[1,16,2,4,16,256]{5,4,2,1,0,3:T(8,128)(2,1)}), bf16[1,16,2,4,16,256]{5,4,2,1,0,3:T(8,128)(2,1)S(1)}, u32[]{:S(2)}, u32[]{:S(2)}) async-start(bf16[1,16,2,4,16,256]{5,4,2,1,0,3:T(8,128)(2,1)} %copy.67), calls=%async_computation.4 | async-start | bytes 2097152 | tf_op jit(solution)/shard_map/all_to_all | solution.py:19
  14.8 47.0 %copy-start = (bf16[2048,256]{1,0:T(8,128)(2,1)S(1)}, bf16[2048,256]{1,0:T(8,128)(2,1)}, u32[]{:S(2)}) copy-start(bf16[2048,256]{1,0:T(8,128)(2,1)} %param.5) | copy-start | bytes 3145732
  61.0 0.8 copy-start.9
  63.4 19.0 %all-to-all-start = ((bf16[1,16,2,4,16,256]{5,1,2,4,0,3:T(8,128)(2,1)}), bf16[1,16,2,4,16,256]{5,1,2,4,0,3:T(8,128)(2,1)}, u32[]{:S(2)}, u32[]{:S(2)}) async-start(bf16[1,16,2,4,16,256]{5,1,2,4,0,3:T(8,128)(2,1)} %bitcast.115), calls=%async_computation | async-start | bytes 2097152 | tf_op jit(solution)/shard_map/all_to_all | solution.py:19
  68.8 1.0 copy-start.21
  70.0 0.8 copy-start.11
  71.2 16.4 %copy-start.20 = (bf16[2,8,128,128]{3,1,2,0:T(8,128)(2,1)S(1)}, bf16[2,8,128,128]{3,1,2,0:T(8,128)(2,1)}, u32[]{:S(2)}) copy-start(bf16[2,8,128,128]{3,1,2,0:T(8,128)(2,1)} %get-tuple-element.6) | copy-start | bytes 1572868
  82.4 18.7 %all-to-all-start.5 = ((bf16[1,16,2,4,16,256]{5,1,2,4,0,3:T(8,128)(2,1)}), bf16[1,16,2,4,16,256]{5,1,2,4,0,3:T(8,128)(2,1)}, u32[]{:S(2)}, u32[]{:S(2)}) async-start(bf16[1,16,2,4,16,256]{5,1,2,4,0,3:T(8,128)(2,1)} %bitcast.111), calls=%async_computation.5 | async-start | bytes 2097152 | tf_op jit(solution)/shard_map/all_to_all | solution.py:19
  87.7 2.5 copy-start.12
  101.2 18.7 %all-to-all-start.1 = ((bf16[1,16,2,4,16,256]{5,1,2,4,0,3:T(8,128)(2,1)}), bf16[1,16,2,4,16,256]{5,1,2,4,0,3:T(8,128)(2,1)}, u32[]{:S(2)}, u32[]{:S(2)}) async-start(bf16[1,16,2,4,16,256]{5,1,2,4,0,3:T(8,128)(2,1)} %bitcast.138), calls=%async_computation.1 | async-start | bytes 2097152 | tf_op jit(solution)/shard_map/all_to_all | solution.py:19
  119.9 2.0 copy-start.22
  119.9 2.0 copy-start.23
  121.9 1.6 copy-start.19
  124.6 18.7 %all-to-all-start.6 = ((bf16[1,16,2,4,16,256]{5,1,2,4,0,3:T(8,128)(2,1)}), bf16[1,16,2,4,16,256]{5,1,2,4,0,3:T(8,128)(2,1)}, u32[]{:S(2)}, u32[]{:S(2)}) async-start(bf16[1,16,2,4,16,256]{5,1,2,4,0,3:T(8,128)(2,1)} %bitcast.140), calls=%async_computation.6 | async-start | bytes 2097152 | tf_op jit(solution)/shard_map/all_to_all | solution.py:19
  132.4 16.2 %copy-start.24 = (s32[4,16]{1,0:T(4,128)S(1)}, s32[4,16]{1,0:T(4,128)}, u32[]{:S(2)}) copy-start(s32[4,16]{1,0:T(4,128)} %param.8) | copy-start | bytes 772
  143.3 18.7 %all-to-all-start.2 = ((bf16[1,16,2,4,16,256]{5,1,2,4,0,3:T(8,128)(2,1)}), bf16[1,16,2,4,16,256]{5,1,2,4,0,3:T(8,128)(2,1)}, u32[]{:S(2)}, u32[]{:S(2)}) async-start(bf16[1,16,2,4,16,256]{5,1,2,4,0,3:T(8,128)(2,1)} %bitcast.137), calls=%async_computation.2 | async-start | bytes 2097152 | tf_op jit(solution)/shard_map/all_to_all | solution.py:19
  148.5 2.9 copy-start.13
  150.4 1.0 copy-start.5
  162.1 20.8 %all-to-all-start.7 = ((bf16[1,16,2,4,16,256]{5,1,2,4,0,3:T(8,128)(2,1)}), bf16[1,16,2,4,16,256]{5,1,2,4,0,3:T(8,128)(2,1)}, u32[]{:S(2)}, u32[]{:S(2)}) async-start(bf16[1,16,2,4,16,256]{5,1,2,4,0,3:T(8,128)(2,1)} %bitcast.136), calls=%async_computation.7 | async-start | bytes 2097152 | tf_op jit(solution)/shard_map/all_to_all | solution.py:19
  167.3 114.4 %reduce-scatter.2.cloned.1.call-start = ((), (), s32[]{:S(2)}) async-start(), calls=%async_computation.10 | async-start | bytes 4718592 | tf_op jit(solution)/shard_map/reduce_scatter | solution.py:79
  180.1 1.0 copy-start.3
  181.6 3.1 %copy-start.2 = (f32[16,128,128]{2,1,0:T(8,128)}, f32[16,128,128]{2,1,0:T(8,128)S(1)}, u32[]{:S(2)}) copy-start(f32[16,128,128]{2,1,0:T(8,128)S(1)} %fusion.17) | copy-start | bytes 3145732
  187.8 6.8 %copy-start.6 = (f32[16,128,128]{2,1,0:T(8,128)}, f32[16,128,128]{2,1,0:T(8,128)S(1)}, u32[]{:S(2)}) copy-start(f32[16,128,128]{2,1,0:T(8,128)S(1)} %copy.75) | copy-start | bytes 3145732
  194.5 1.2 copy-start.4
  198.4 7.0 %copy-start.1 = (f32[16,128,128]{2,1,0:T(8,128)S(1)}, f32[16,128,128]{2,1,0:T(8,128)}, u32[]{:S(2)}) copy-start(f32[16,128,128]{2,1,0:T(8,128)} %fusion.16) | copy-start | bytes 3145732
  198.4 18.2 %all-to-all-start.3 = ((bf16[1,16,2,4,16,256]{5,1,2,4,0,3:T(8,128)(2,1)}), bf16[1,16,2,4,16,256]{5,1,2,4,0,3:T(8,128)(2,1)}, u32[]{:S(2)}, u32[]{:S(2)}) async-start(bf16[1,16,2,4,16,256]{5,1,2,4,0,3:T(8,128)(2,1)} %bitcast.139), calls=%async_computation.3 | async-start | bytes 2097152 | tf_op jit(solution)/shard_map/all_to_all | solution.py:19
  206.6 2.5 copy-start.7
  210.2 8.3 %copy-start.10 = (bf16[2,8,128,128]{3,2,1,0:T(8,128)(2,1)S(1)}, bf16[2,8,128,128]{3,2,1,0:T(8,128)(2,1)}, u32[]{:S(2)}) copy-start(bf16[2,8,128,128]{3,2,1,0:T(8,128)(2,1)} %copy-done.9) | copy-start | bytes 1572868
  216.5 2.0 copy-start.14
  218.5 2.7 copy-start.16
  218.5 2.7 copy-start.17
  218.5 2.7 copy-start.18
  219.9 2.2 copy-start.8
  219.9 2.5 copy-start.15
Sparse Core Ops, SparseCore 0:
  10.2 47.9 all-gather.1
  194.7 86.9 reduce-scatter.1
where the time goes:
time: 295 us; the launch traced here: 290 us
  waiting for transfers between devices  155 us (53%)
  local copies, waits for them, and re-layouts  52.9 us (18%)
  starting transfers between devices  40.1 us (14%)
  matrix products  17.1 us (6%)
  between operations  14.3 us (5%)
  other arithmetic  10.6 us (4%)
    reduce_scatter x1, waiting for transfers between devices, body(): lax.psum_scatter(code_values, 'dev', scatter_dimension=2, tiled=True)  57.3 us
    all_to_all x8, waiting for transfers between devices, regroup(): lax.all_to_all(shaped, 'ma', split_axis=3, concat_axis=3, tiled=True)  54.1 us
    all_gather x1, waiting for transfers between devices, body(): gathered = lax.all_gather(factors, 'dev', axis=2, tiled=True)  43.4 us
    all_to_all x8, starting transfers between devices, regroup(): lax.all_to_all(shaped, 'ma', split_axis=3, concat_axis=3, tiled=True)  40.1 us
    another operation x8, local copies, waits for them, and re-layouts, body(): jnp.stack([gradient_zero, gradient_one, gradient_two, gradient_three])  14.7 us
    all_to_all x7, local copies, waits for them, and re-layouts, regroup(): lax.all_to_all(shaped, 'ma', split_axis=3, concat_axis=3, tiled=True)  12.3 us
    unnamed x55, local copies, waits for them, and re-layouts  11.8 us
    dot_general x4, matrix products, outer_sum(): jnp.einsum('nct,ndt->ncd', left, right, preferred_element_type=jnp.float32)  8.22 us
  transfers between devices with their start and end apart: 10, of which 8 were waited for; matrix products, arithmetic and copies ran while one was open for 19% of the time, Pallas kernels for 0%

commit v1 on v0

v1 whole, which is shorter than its diff:
```python
import functools

import jax
import jax.numpy as jnp
from jax import lax
from jax.experimental import pallas as pl
from jax.experimental.pallas import tpu as pltpu
from jax.sharding import PartitionSpec as P

B = 128
LANES = 128
LIMIT = 127.0
C0 = 0.7978845608028654
C1 = 0.044715
F32 = jnp.float32
BF16 = jnp.bfloat16
ORDER = (0, 3, 1, 2)
COT, ONE, DTHIRD, PRE, DSECOND, TWO, DFIRST, LAST = range(8)


def dot(a, b):
    return lax.dot_general(a, b, (((1,), (0,)), ((), ())), preferred_element_type=F32)


def dot_nt(a, b):
    return lax.dot_general(a, b, (((1,), (1,)), ((), ())), preferred_element_type=F32)


def kernel(
    G, M, inp, cot, fac, expo, err, out, igrad, gmean, nerr,
    x_v, c_v, e_v, hid, rx, tx, sf, gs, wg, w_n, w_t, cod, crx, o_v, g_v, m_v, n_v,
    ld, st, xs, xr, ws, wr, cs_s, cs_r,
):
    F, nb, S = fac.shape
    H = x_v.shape[0]
    NBT = M * nb
    U = B // NBT
    CS = S // B
    seg = nb * U * nb
    ma = lax.axis_index("ma")
    dev = lax.axis_index("dev")

    def lanes(h):
        return slice(h * LANES, (h + 1) * LANES)

    loads = []
    for h in range(H):
        loads.append(pltpu.make_async_copy(cot.at[:, lanes(h)], c_v.at[h], ld.at[h]))
    for h in range(H):
        loads.append(pltpu.make_async_copy(inp.at[:, lanes(h)], x_v.at[h], ld.at[H + h]))
    loads.append(pltpu.make_async_copy(err.at[0], e_v, ld.at[2 * H]))
    own = pltpu.make_async_copy(fac, wg.at[:, dev], ld.at[2 * H + 1])
    for cp in loads:
        cp.start()
    own.start()

    barrier = pltpu.get_barrier_semaphore()
    for d in range(1, M):
        pl.semaphore_signal(barrier, inc=1, device_id={"ma": lax.rem(ma + d, M)}, device_id_type=pl.DeviceIdType.MESH)

    def greet(d, _):
        pl.semaphore_signal(barrier, inc=1, device_id={"dev": lax.rem(dev + d, G)}, device_id_type=pl.DeviceIdType.MESH)
        return 0

    lax.fori_loop(1, G, greet, 0)

    def w_copy(f, d, slot):
        return pltpu.make_async_remote_copy(
            src_ref=fac.at[f], dst_ref=wg.at[f, slot], send_sem=ws.at[f, d], recv_sem=wr.at[f, d],
            device_id={"dev": lax.rem(dev + d, G)}, device_id_type=pl.DeviceIdType.MESH,
        )

    def x_copy(k, h, d, src):
        return pltpu.make_async_remote_copy(
            src_ref=tx.at[k, h, d - 1], dst_ref=rx.at[k, h, :, pl.ds(pl.multiple_of(src * nb, nb), nb), :],
            send_sem=xs.at[k, h, d], recv_sem=xr.at[k, h, d],
            device_id={"ma": lax.rem(ma + d, M)}, device_id_type=pl.DeviceIdType.MESH,
        )

    def c_copy(f, d, slot):
        return pltpu.make_async_remote_copy(
            src_ref=cod.at[f, d], dst_ref=crx.at[f, slot], send_sem=cs_s.at[f, d], recv_sem=cs_r.at[f, d],
            device_id={"dev": lax.rem(dev + d, G)}, device_id_type=pl.DeviceIdType.MESH,
        )

    def spread(i, value):
        for u in range(U):
            sf[pl.ds(u * nb + i, NBT, stride=U * nb), :] = value[u * NBT:(u + 1) * NBT]

    def part(m):
        rows = sf[pl.ds(pl.multiple_of(m * seg, seg), seg), :]
        return rows.astype(BF16).reshape(nb * U, nb, LANES)

    def pack(k, h):
        for d in range(1, M):
            tx[k, h, d - 1] = part(lax.rem(ma + d, M))

    def launch(k, h):
        for d in range(1, M):
            x_copy(k, h, d, ma).start()

    def keep(k, h):
        rx[k, h, :, pl.ds(pl.multiple_of(ma * nb, nb), nb), :] = part(ma)

    def send(k, h):
        for d in range(1, M):
            tx[k, h, d - 1] = part(lax.rem(ma + d, M))
            x_copy(k, h, d, ma).start()
        keep(k, h)

    def arrive(k, h):
        for d in range(1, M):
            x_copy(k, h, d, lax.rem(ma + M - d, M)).wait_recv()

    def block(k, h, i):
        return rx[k, h, pl.ds(i * U, U)].reshape(B, LANES)

    def rows_of(ref, h, i):
        return ref[h, pl.ds(pl.multiple_of(i * B, B), B), :]

    def each(fn, unroll=4):
        def step(i, _):
            fn(i)
            return 0

        lax.fori_loop(0, nb, step, 0, unroll=unroll)

    def weights(f):
        def arrived(d, _):
            w_copy(f, d, lax.rem(dev + G - d, G)).wait_recv()
            return 0

        lax.fori_loop(1, G, arrived, 0)

        def widen(g, _):
            for c in range(CS):
                at = pl.multiple_of((g * CS + c) * nb, nb)
                gs[pl.ds(at, nb), :] = wg[f, g, :, c * B:(c + 1) * B].astype(F32)
            return 0

        lax.fori_loop(0, G, widen, 0)

        def take(n):
            w = gs[pl.ds(n, B, stride=nb), :]
            w_n[f, n] = w.astype(BF16)
            w_t[f, n] = w.T.astype(BF16)

        each(take, 2)

    def gradient(f, left, right):
        def one(n):
            total = dot_nt(left(0, n), right(0, n))
            for h in range(1, H):
                total = total + dot_nt(left(h, n), right(h, n))
            gs[pl.ds(n, B, stride=nb), :] = total

        each(one)
        row = lax.broadcasted_iota(jnp.int32, (nb, B), 0)
        power = jnp.zeros((nb, B), jnp.int32)
        for n in range(nb):
            power = jnp.where(row == n, expo[f, n], power)
        scale = jnp.left_shift(jnp.ones_like(power), -power).astype(F32)
        inverse = jnp.left_shift(jnp.ones_like(power), 24 + power).astype(F32) * (2.0 ** -24)

        def quantize(g, put):
            for c in range(CS):
                col = pl.ds(pl.multiple_of((g * CS + c) * B, B), B)
                total = gs[pl.ds(pl.multiple_of((g * CS + c) * nb, nb), nb), :] + e_v[f, :, col].astype(F32)
                code = jnp.clip(total * scale, -LIMIT, LIMIT)
                n_v[f, :, col] = (total - code * inverse).astype(BF16)
                put(c, code.astype(BF16))

        def away(d, _):
            def put(c, code):
                cod[f, d, :, c * B:(c + 1) * B] = code

            quantize(lax.rem(dev + d, G), put)
            c_copy(f, d, dev).start()
            return 0

        lax.fori_loop(1, G, away, 0)

        def put_own(c, code):
            crx[f, dev, :, c * B:(c + 1) * B] = code

        quantize(dev, put_own)
        pltpu.make_async_copy(n_v.at[f], nerr.at[0, f], st.at[f]).start()
        return inverse

    def spread_cot(h):
        each(lambda i: spread(i, rows_of(c_v, h, i).astype(F32)))

    loads[0].wait()
    spread_cot(0)
    pack(COT, 0)
    keep(COT, 0)
    pl.semaphore_wait(barrier, M - 1 + G - 1)
    launch(COT, 0)
    for f in ORDER:
        def push(d, _, f=f):
            w_copy(f, d, dev).start()
            return 0

        lax.fori_loop(1, G, push, 0)
    for h in range(1, H):
        loads[h].wait()
        spread_cot(h)
        send(COT, h)

    own.wait()
    for h in range(H):
        loads[H + h].wait()
    weights(0)
    for h in range(H):
        each(lambda i: spread(i, dot(w_t[0, i], rows_of(x_v, h, i))))
        send(ONE, h)
    weights(3)
    for h in range(H):
        arrive(COT, h)
        each(lambda i: spread(i, dot(w_n[3, i], block(COT, h, i))))
        send(DTHIRD, h)
    weights(1)
    for h in range(H):
        arrive(ONE, h)
        each(lambda i: spread(i, dot(w_t[1, i], block(ONE, h, i))))
        send(PRE, h)
    weights(2)
    for h in range(H):
        arrive(DTHIRD, h)
    for h in range(H):
        arrive(PRE, h)

        def middle(i):
            v = block(PRE, h, i).astype(F32)
            square = v * v
            t = jnp.tanh(C0 * (v + C1 * (square * v)))
            half = 0.5 * (1.0 + t)
            hid[h, pl.ds(pl.multiple_of(i * B, B), B), :] = (v * half).astype(BF16)
            slope = half + 0.5 * v * (1.0 - t * t) * (C0 * (1.0 + 3.0 * C1 * square))
            spread(i, dot(w_n[2, i], block(DTHIRD, h, i)) * slope)

        each(middle, 2)
        send(DSECOND, h)
    for h in range(H):
        each(lambda i: spread(i, dot(w_t[2, i], rows_of(hid, h, i))))
        send(TWO, h)
    loads[2 * H].wait()
    inverses = {}
    inverses[2] = gradient(2, lambda h, n: rows_of(hid, h, n), lambda h, n: block(DTHIRD, h, n))
    for h in range(H):
        arrive(DSECOND, h)
        each(lambda i: spread(i, dot(w_n[1, i], block(DSECOND, h, i))))
        send(DFIRST, h)
    inverses[1] = gradient(1, lambda h, n: block(ONE, h, n), lambda h, n: block(DSECOND, h, n))
    for h in range(H):
        arrive(TWO, h)
        each(lambda i: spread(i, dot(w_t[3, i], block(TWO, h, i))))
        send(LAST, h)
    inverses[3] = gradient(3, lambda h, n: block(TWO, h, n), lambda h, n: block(COT, h, n))
    for h in range(H):
        arrive(DFIRST, h)
    inverses[0] = gradient(0, lambda h, n: rows_of(x_v, h, n), lambda h, n: block(DFIRST, h, n))
    stores = []
    for h in range(H):
        def back(i):
            value = rows_of(c_v, h, i).astype(F32) + dot(w_n[0, i], block(DFIRST, h, i))
            g_v[h, pl.ds(pl.multiple_of(i * B, B), B), :] = value.astype(BF16)

        each(back)
        stores.append(pltpu.make_async_copy(g_v.at[h], igrad.at[:, lanes(h)], st.at[2 * F + h]))
        stores[-1].start()

    def mean(f):
        def arrived(d, _):
            c_copy(f, d, lax.rem(dev + G - d, G)).wait_recv()
            return 0

        lax.fori_loop(1, G, arrived, 0)

        def column(c, _):
            col = pl.ds(pl.multiple_of(c * B, B), B)
            total = crx[f, 0, :, col].astype(F32)
            for g in range(1, G):
                total = total + crx[f, g, :, col].astype(F32)
            m_v[f, :, col] = total * inverses[f] / G
            return 0

        lax.fori_loop(0, CS, column, 0)
        stores.append(pltpu.make_async_copy(m_v.at[f], gmean.at[f], st.at[F + f]))
        stores[-1].start()

    for f in (2, 1, 3):
        mean(f)
    for h in range(H):
        arrive(LAST, h)

        def finish(i):
            value = rows_of(x_v, h, i).astype(F32) + block(LAST, h, i).astype(F32)
            o_v[h, pl.ds(pl.multiple_of(i * B, B), B), :] = value.astype(BF16)

        each(finish)
        stores.append(pltpu.make_async_copy(o_v.at[h], out.at[:, lanes(h)], st.at[2 * F + H + h]))
        stores[-1].start()
    mean(0)
    for f in range(F):
        pltpu.make_async_copy(n_v.at[f], nerr.at[0, f], st.at[f]).wait()
    for cp in stores:
        cp.wait()

    def sent(d, _):
        for f in range(F):
            w_copy(f, d, dev).wait_send()
            c_copy(f, d, dev).wait_send()
        return 0

    lax.fori_loop(1, G, sent, 0)
    for k in range(8):
        for h in range(H):
            for d in range(1, M):
                x_copy(k, h, d, ma).wait_send()


def step(G, M, inp, cot, fac, expo, err):
    F, nb, S = fac.shape
    R, T = inp.shape
    H = T // LANES
    NBT = M * nb
    U = B // NBT
    hbm = pl.BlockSpec(memory_space=pl.ANY)
    return pl.pallas_call(
        functools.partial(kernel, G, M),
        out_shape=(
            jax.ShapeDtypeStruct((R, T), BF16),
            jax.ShapeDtypeStruct((R, T), BF16),
            jax.ShapeDtypeStruct(fac.shape, F32),
            jax.ShapeDtypeStruct(err.shape, BF16),
        ),
        in_specs=[hbm, hbm, hbm, pl.BlockSpec(memory_space=pltpu.SMEM), hbm],
        out_specs=(hbm,) * 4,
        scratch_shapes=[
            pltpu.VMEM((H, R, LANES), BF16),
            pltpu.VMEM((H, R, LANES), BF16),
            pltpu.VMEM((F, nb, B * B), BF16),
            pltpu.VMEM((H, R, LANES), BF16),
            pltpu.VMEM((8, H, nb * U, NBT, LANES), BF16),
            pltpu.VMEM((8, H, M - 1, nb * U, nb, LANES), BF16),
            pltpu.VMEM((R, LANES), F32),
            pltpu.VMEM((R, LANES), F32),
            pltpu.VMEM((F, G, nb, S), BF16),
            pltpu.VMEM((F, nb, B, B), BF16),
            pltpu.VMEM((F, nb, B, B), BF16),
            pltpu.VMEM((F, G, nb, S), BF16),
            pltpu.VMEM((F, G, nb, S), BF16),
            pltpu.VMEM((H, R, LANES), BF16),
            pltpu.VMEM((H, R, LANES), BF16),
            pltpu.VMEM((F, nb, S), F32),
            pltpu.VMEM((F, nb, B * B), BF16),
            pltpu.SemaphoreType.DMA((2 * H + 2,)),
            pltpu.SemaphoreType.DMA((2 * F + 2 * H,)),
            pltpu.SemaphoreType.DMA((8, H, M)),
            pltpu.SemaphoreType.DMA((8, H, M)),
            pltpu.SemaphoreType.DMA((F, G)),
            pltpu.SemaphoreType.DMA((F, G)),
            pltpu.SemaphoreType.DMA((F, G)),
            pltpu.SemaphoreType.DMA((F, G)),
        ],
        compiler_params=pltpu.CompilerParams(
            collective_id=0, has_side_effects=True, vmem_limit_bytes=60 * 1024 * 1024
        ),
    )(inp, cot, fac, expo, err)


def solution(mesh):
    G, M = mesh.shape["dev"], mesh.shape["ma"]
    in_specs = (
        P("ma", "dev"),
        P("ma", "dev"),
        P(None, "ma", "dev"),
        P(None, "ma"),
        P("dev", None, "ma", None),
    )
    out_specs = (P("ma", "dev"), P("ma", "dev"), P(None, "ma", "dev"), P("dev", None, "ma", None))
    return jax.shard_map(
        functools.partial(step, G, M), mesh=mesh, in_specs=in_specs, out_specs=out_specs, check_vma=False
    )
```

time: 295 us -> 122 us (0.41); the launches traced: 290 us -> 122 us
  waiting for transfers between devices: 155 us -> 0 us
  Pallas kernels: 0 us -> 116 us
  local copies, waits for them, and re-layouts: 52.9 us -> 5.51 us
  starting transfers between devices: 40.1 us -> 0 us
  matrix products: 17.1 us -> 0 us
  between operations: 14.3 us -> 0.67 us
  other arithmetic: 10.6 us -> 0 us
    pallas_call x0 -> x1, Pallas kernels: none -> 116 us  [step(): pl.pallas_call(functools.partial(kernel, G, M), out_shape=(jax.ShapeDtype...]
    reduce_scatter x1 -> x0, waiting for transfers between devices: 57.3 us -> none  [body(): lax.psum_scatter(code_values, 'dev', scatter_dimension=2, tiled=True)]
    all_to_all x8 -> x0, waiting for transfers between devices: 54.1 us -> none  [regroup(): lax.all_to_all(shaped, 'ma', split_axis=3, concat_axis=3, tiled=True)]
    all_gather x1 -> x0, waiting for transfers between devices: 43.4 us -> none  [body(): gathered = lax.all_gather(factors, 'dev', axis=2, tiled=True)]
    all_to_all x8 -> x0, starting transfers between devices: 40.1 us -> none  [regroup(): lax.all_to_all(shaped, 'ma', split_axis=3, concat_axis=3, tiled=True)]
    another operation x15 -> x0, local copies, waits for them, and re-layouts: 22.5 us -> none  [the longest x8 14.7 us: body(): jnp.stack([gradient_zero, gradient_one, gradient_two, gradient_three])]
    dot_general x12 -> x0, matrix products: 17.1 us -> none  [the longest x4 8.22 us: outer_sum(): jnp.einsum('nct,ndt->ncd', left, right, preferred_element_type=jnp.float32)]
    all_to_all x7 -> x0, local copies, waits for them, and re-layouts: 12.3 us -> none  [regroup(): lax.all_to_all(shaped, 'ma', split_axis=3, concat_axis=3, tiled=True)]
  transfers between devices with their start and end apart: 10 -> 0, of which waited for: 8 -> 0; matrix products, arithmetic and copies ran while one was open for 19% -> 0% of each run, Pallas kernels for 0% -> 0%
where the time goes in v1:
time: 122 us
  Pallas kernels  116 us (95%)
  local copies, waits for them, and re-layouts  5.51 us (5%)
    pallas_call x1, Pallas kernels, step(): pl.pallas_call(functools.partial(kernel, G, M), out_shape=(jax.ShapeDtype...  116 us
    unnamed x10, local copies, waits for them, and re-layouts  5.51 us

profile of v1, /device:TPU:25, one launch (start us, length us, event | category | flops | bytes accessed | tf_op | source)
XLA Modules:
  0.0 122.0 jit_solution(14088356189729018840)
XLA Ops:
  0.6 115.8 %shard_map.84 = (bf16[2048,256]{1,0:T(8,128)(2,1)}, bf16[2048,256]{1,0:T(8,128)(2,1)}, f32[4,16,2048]{2,1,0:T(8,128)}, bf16[1,4,16,16384]{3,2,1,0:T(8,128)(2,1)}) custom-call(bf16[2048,256]{1,0:T(8,128)(2,1)} %inp.1, bf16[2048,256]{1,0:T(8,128)(2,1)} %cot.1, bf16[4,16,2048]{2,1,0:T(8,128)(2,1)} %fac.1, s32[4,16]{1,0:T(4,128)} %expo.1, ...), custom_call_target="tpu_custom_call" | custom-call | tf_op jit(solution)/shard_map/pallas_call | solution.py:330
  116.5 0.0 copy-start.1
  116.5 0.0 copy-start.2
  116.5 0.0 copy-start
  116.5 2.4 %copy.13 = bf16[2048,256]{1,0:T(8,128)(2,1)} copy(bf16[2048,256]{1,0:T(8,128)(2,1)} %get-tuple-element.8) | data formatting | bytes 2097152
  118.9 0.0 copy-done.1
  118.9 1.0 copy.14
  119.9 0.0 copy-done.2
  119.9 0.8 copy.15
  120.7 0.0 copy-done
  120.7 1.3 %copy.16 = bf16[1,4,16,16384]{3,2,1,0:T(8,128)(2,1)} copy(bf16[1,4,16,16384]{3,2,1,0:T(8,128)(2,1)S(1)} %copy-done) | data formatting | bytes 4194304
Async XLA Ops:
  116.5 2.4 %copy-start.1 = (bf16[2048,256]{1,0:T(8,128)(2,1)S(1)}, bf16[2048,256]{1,0:T(8,128)(2,1)}, u32[]{:S(2)}) copy-start(bf16[2048,256]{1,0:T(8,128)(2,1)} %get-tuple-element.9) | copy-start | bytes 3145732
  116.5 3.4 %copy-start.2 = (f32[4,16,2048]{2,1,0:T(8,128)S(1)}, f32[4,16,2048]{2,1,0:T(8,128)}, u32[]{:S(2)}) copy-start(f32[4,16,2048]{2,1,0:T(8,128)} %get-tuple-element.10) | copy-start | bytes 1572868
  116.5 4.2 %copy-start = (bf16[1,4,16,16384]{3,2,1,0:T(8,128)(2,1)S(1)}, bf16[1,4,16,16384]{3,2,1,0:T(8,128)(2,1)}, u32[]{:S(2)}) copy-start(bf16[1,4,16,16384]{3,2,1,0:T(8,128)(2,1)} %get-tuple-element.11) | copy-start | bytes 6291460

commit v2 on v1

--- a/solution.py
+++ b/solution.py
@@ -29,7 +29,7 @@
 def kernel(
     G, M, inp, cot, fac, expo, err, out, igrad, gmean, nerr,
     x_v, c_v, e_v, hid, rx, tx, sf, gs, wg, w_n, w_t, cod, crx, o_v, g_v, m_v, n_v,
-    ld, st, xs, xr, ws, wr, cs_s, cs_r,
+    ld, st, xs, xr, ws, wr, ps, pr, cs_s, cs_r,
 ):
     F, nb, S = fac.shape
     H = x_v.shape[0]
@@ -39,6 +39,8 @@
     seg = nb * U * nb
     ma = lax.axis_index("ma")
     dev = lax.axis_index("dev")
+    half_group = G // 2
+    partner = dev + 1 - 2 * lax.rem(dev, 2)
 
     def lanes(h):
         return slice(h * LANES, (h + 1) * LANES)
@@ -67,8 +69,23 @@
     def w_copy(f, d, slot):
         return pltpu.make_async_remote_copy(
             src_ref=fac.at[f], dst_ref=wg.at[f, slot], send_sem=ws.at[f, d], recv_sem=wr.at[f, d],
-            device_id={"dev": lax.rem(dev + d, G)}, device_id_type=pl.DeviceIdType.MESH,
+            device_id={"dev": lax.rem(dev + 2 * d, G)}, device_id_type=pl.DeviceIdType.MESH,
         )
+
+    def p_copy(f, d, source, slot):
+        return pltpu.make_async_remote_copy(
+            src_ref=source, dst_ref=wg.at[f, slot], send_sem=ps.at[f, d], recv_sem=pr.at[f, d],
+            device_id={"dev": partner}, device_id_type=pl.DeviceIdType.MESH,
+        )
+
+    def forward(f):
+        def one(d, _):
+            slot = lax.rem(dev + G - 2 * d, G)
+            w_copy(f, d, slot).wait_recv()
+            p_copy(f, d, wg.at[f, slot], slot).start()
+            return 0
+
+        lax.fori_loop(1, half_group, one, 0)
 
     def x_copy(k, h, d, src):
         return pltpu.make_async_remote_copy(
@@ -127,10 +144,11 @@
 
     def weights(f):
         def arrived(d, _):
-            w_copy(f, d, lax.rem(dev + G - d, G)).wait_recv()
-            return 0
-
-        lax.fori_loop(1, G, arrived, 0)
+            slot = lax.rem(partner + G - 2 * d, G)
+            p_copy(f, d, wg.at[f, slot], slot).wait_recv()
+            return 0
+
+        lax.fori_loop(0, half_group, arrived, 0)
 
         def widen(g, _):
             for c in range(CS):
@@ -201,7 +219,8 @@
             w_copy(f, d, dev).start()
             return 0
 
-        lax.fori_loop(1, G, push, 0)
+        lax.fori_loop(1, half_group, push, 0)
+        p_copy(f, 0, fac.at[f], dev).start()
     for h in range(1, H):
         loads[h].wait()
         spread_cot(h)
@@ -210,20 +229,27 @@
     own.wait()
     for h in range(H):
         loads[H + h].wait()
+    forward(0)
     weights(0)
     for h in range(H):
         each(lambda i: spread(i, dot(w_t[0, i], rows_of(x_v, h, i))))
         send(ONE, h)
+        if h == 0:
+            forward(3)
     weights(3)
     for h in range(H):
         arrive(COT, h)
         each(lambda i: spread(i, dot(w_n[3, i], block(COT, h, i))))
         send(DTHIRD, h)
+        if h == 0:
+            forward(1)
     weights(1)
     for h in range(H):
         arrive(ONE, h)
         each(lambda i: spread(i, dot(w_t[1, i], block(ONE, h, i))))
         send(PRE, h)
+        if h == 0:
+            forward(2)
     weights(2)
     for h in range(H):
         arrive(DTHIRD, h)
@@ -309,11 +335,21 @@
 
     def sent(d, _):
         for f in range(F):
-            w_copy(f, d, dev).wait_send()
             c_copy(f, d, dev).wait_send()
         return 0
 
     lax.fori_loop(1, G, sent, 0)
+
+    def handed(d, _):
+        for f in range(F):
+            w_copy(f, d, dev).wait_send()
+            slot = lax.rem(dev + G - 2 * d, G)
+            p_copy(f, d, wg.at[f, slot], slot).wait_send()
+        return 0
+
+    lax.fori_loop(1, half_group, handed, 0)
+    for f in range(F):
+        p_copy(f, 0, fac.at[f], dev).wait_send()
     for k in range(8):
         for h in range(H):
             for d in range(1, M):
@@ -359,8 +395,10 @@
             pltpu.SemaphoreType.DMA((2 * F + 2 * H,)),
             pltpu.SemaphoreType.DMA((8, H, M)),
             pltpu.SemaphoreType.DMA((8, H, M)),
-            pltpu.SemaphoreType.DMA((F, G)),
-            pltpu.SemaphoreType.DMA((F, G)),
+            pltpu.SemaphoreType.DMA((F, G // 2)),
+            pltpu.SemaphoreType.DMA((F, G // 2)),
+            pltpu.SemaphoreType.DMA((F, G // 2)),
+            pltpu.SemaphoreType.DMA((F, G // 2)),
             pltpu.SemaphoreType.DMA((F, G)),
             pltpu.SemaphoreType.DMA((F, G)),
         ],

time: 122 us -> 116 us (0.951)
  Pallas kernels: 116 us -> 109 us
    pallas_call x1, Pallas kernels: 116 us -> 109 us  [step(): pl.pallas_call(functools.partial(kernel, G, M), out_shape=(jax.ShapeDtype...]
where the time goes in v2:
time: 116 us; the launch traced here: 115 us
  Pallas kernels  109 us (94%)
  local copies, waits for them, and re-layouts  5.51 us (5%)
    pallas_call x1, Pallas kernels, step(): pl.pallas_call(functools.partial(kernel, G, M), out_shape=(jax.ShapeDtype...  109 us
    unnamed x10, local copies, waits for them, and re-layouts  5.51 us

profile of v2, /device:TPU:25, one launch (start us, length us, event | category | flops | bytes accessed | tf_op | source)
XLA Modules:
  0.0 115.3 jit_solution(7569298593979109413)
XLA Ops:
  0.6 109.1 %shard_map.84 = (bf16[2048,256]{1,0:T(8,128)(2,1)}, bf16[2048,256]{1,0:T(8,128)(2,1)}, f32[4,16,2048]{2,1,0:T(8,128)}, bf16[1,4,16,16384]{3,2,1,0:T(8,128)(2,1)}) custom-call(bf16[2048,256]{1,0:T(8,128)(2,1)} %inp.1, bf16[2048,256]{1,0:T(8,128)(2,1)} %cot.1, bf16[4,16,2048]{2,1,0:T(8,128)(2,1)} %fac.1, s32[4,16]{1,0:T(4,128)} %expo.1, ...), custom_call_target="tpu_custom_call" | custom-call | tf_op jit(solution)/shard_map/pallas_call | solution.py:366
  109.7 0.0 copy-start.1
  109.7 0.0 copy-start.2
  109.8 0.0 copy-start
  109.8 2.4 %copy.13 = bf16[2048,256]{1,0:T(8,128)(2,1)} copy(bf16[2048,256]{1,0:T(8,128)(2,1)} %get-tuple-element.8) | data formatting | bytes 2097152
  112.2 0.0 copy-done.1
  112.2 1.0 copy.14
  113.2 0.0 copy-done.2
  113.2 0.8 copy.15
  113.9 0.0 copy-done
  113.9 1.3 %copy.16 = bf16[1,4,16,16384]{3,2,1,0:T(8,128)(2,1)} copy(bf16[1,4,16,16384]{3,2,1,0:T(8,128)(2,1)S(1)} %copy-done) | data formatting | bytes 4194304
Async XLA Ops:
  109.7 2.4 %copy-start.1 = (bf16[2048,256]{1,0:T(8,128)(2,1)S(1)}, bf16[2048,256]{1,0:T(8,128)(2,1)}, u32[]{:S(2)}) copy-start(bf16[2048,256]{1,0:T(8,128)(2,1)} %get-tuple-element.9) | copy-start | bytes 3145732
  109.7 3.4 %copy-start.2 = (f32[4,16,2048]{2,1,0:T(8,128)S(1)}, f32[4,16,2048]{2,1,0:T(8,128)}, u32[]{:S(2)}) copy-start(f32[4,16,2048]{2,1,0:T(8,128)} %get-tuple-element.10) | copy-start | bytes 1572868
  109.8 4.2 %copy-start = (bf16[1,4,16,16384]{3,2,1,0:T(8,128)(2,1)S(1)}, bf16[1,4,16,16384]{3,2,1,0:T(8,128)(2,1)}, u32[]{:S(2)}) copy-start(bf16[1,4,16,16384]{3,2,1,0:T(8,128)(2,1)} %get-tuple-element.11) | copy-start | bytes 6291460

commit v3 on v2

--- a/solution.py
+++ b/solution.py
@@ -29,7 +29,7 @@
 def kernel(
     G, M, inp, cot, fac, expo, err, out, igrad, gmean, nerr,
     x_v, c_v, e_v, hid, rx, tx, sf, gs, wg, w_n, w_t, cod, crx, o_v, g_v, m_v, n_v,
-    ld, st, xs, xr, ws, wr, ps, pr, cs_s, cs_r,
+    ld, st, xs, xr, ws, wr, ps, pr, cs_s, cs_r, qs, qr,
 ):
     F, nb, S = fac.shape
     H = x_v.shape[0]
@@ -94,11 +94,29 @@
             device_id={"ma": lax.rem(ma + d, M)}, device_id_type=pl.DeviceIdType.MESH,
         )
 
-    def c_copy(f, d, slot):
+    def q_copy(f, d):
         return pltpu.make_async_remote_copy(
-            src_ref=cod.at[f, d], dst_ref=crx.at[f, slot], send_sem=cs_s.at[f, d], recv_sem=cs_r.at[f, d],
-            device_id={"dev": lax.rem(dev + d, G)}, device_id_type=pl.DeviceIdType.MESH,
+            src_ref=cod.at[f, d], dst_ref=crx.at[f, half_group + d], send_sem=qs.at[f, d], recv_sem=qr.at[f, d],
+            device_id={"dev": partner}, device_id_type=pl.DeviceIdType.MESH,
         )
+
+    def c_copy(f, d):
+        return pltpu.make_async_remote_copy(
+            src_ref=cod.at[f, half_group + d], dst_ref=crx.at[f, d], send_sem=cs_s.at[f, d], recv_sem=cs_r.at[f, d],
+            device_id={"dev": lax.rem(dev + 2 * d, G)}, device_id_type=pl.DeviceIdType.MESH,
+        )
+
+    def combine(f):
+        def one(d, _):
+            q_copy(f, d).wait_recv()
+            both = cod[f, half_group + d].astype(F32) + crx[f, half_group + d].astype(F32)
+            cod[f, half_group + d] = both.astype(BF16)
+            c_copy(f, d).start()
+            return 0
+
+        lax.fori_loop(1, half_group, one, 0)
+        q_copy(f, 0).wait_recv()
+        crx[f, 0] = (cod[f, half_group].astype(F32) + crx[f, half_group].astype(F32)).astype(BF16)
 
     def spread(i, value):
         for u in range(U):
@@ -188,20 +206,25 @@
                 n_v[f, :, col] = (total - code * inverse).astype(BF16)
                 put(c, code.astype(BF16))
 
-        def away(d, _):
-            def put(c, code):
-                cod[f, d, :, c * B:(c + 1) * B] = code
-
-            quantize(lax.rem(dev + d, G), put)
-            c_copy(f, d, dev).start()
-            return 0
-
-        lax.fori_loop(1, G, away, 0)
-
-        def put_own(c, code):
-            crx[f, dev, :, c * B:(c + 1) * B] = code
-
-        quantize(dev, put_own)
+        def put(slot):
+            def store(c, code):
+                cod[f, slot, :, c * B:(c + 1) * B] = code
+
+            return store
+
+        def away(step, _):
+            d = lax.rem(step + 1, half_group)
+            quantize(lax.rem(partner + 2 * d, G), put(d))
+            q_copy(f, d).start()
+            return 0
+
+        lax.fori_loop(0, half_group, away, 0)
+
+        def stay(d, _):
+            quantize(lax.rem(dev + 2 * d, G), put(half_group + d))
+            return 0
+
+        lax.fori_loop(0, half_group, stay, 0)
         pltpu.make_async_copy(n_v.at[f], nerr.at[0, f], st.at[f]).start()
         return inverse
 
@@ -277,15 +300,19 @@
         arrive(DSECOND, h)
         each(lambda i: spread(i, dot(w_n[1, i], block(DSECOND, h, i))))
         send(DFIRST, h)
+    combine(2)
     inverses[1] = gradient(1, lambda h, n: block(ONE, h, n), lambda h, n: block(DSECOND, h, n))
     for h in range(H):
         arrive(TWO, h)
         each(lambda i: spread(i, dot(w_t[3, i], block(TWO, h, i))))
         send(LAST, h)
+    combine(1)
     inverses[3] = gradient(3, lambda h, n: block(TWO, h, n), lambda h, n: block(COT, h, n))
+    combine(3)
     for h in range(H):
         arrive(DFIRST, h)
     inverses[0] = gradient(0, lambda h, n: rows_of(x_v, h, n), lambda h, n: block(DFIRST, h, n))
+    combine(0)
     stores = []
     for h in range(H):
         def back(i):
@@ -298,15 +325,15 @@
 
     def mean(f):
         def arrived(d, _):
-            c_copy(f, d, lax.rem(dev + G - d, G)).wait_recv()
-            return 0
-
-        lax.fori_loop(1, G, arrived, 0)
+            c_copy(f, d).wait_recv()
+            return 0
+
+        lax.fori_loop(1, half_group, arrived, 0)
 
         def column(c, _):
             col = pl.ds(pl.multiple_of(c * B, B), B)
             total = crx[f, 0, :, col].astype(F32)
-            for g in range(1, G):
+            for g in range(1, half_group):
                 total = total + crx[f, g, :, col].astype(F32)
             m_v[f, :, col] = total * inverses[f] / G
             return 0
@@ -333,16 +360,11 @@
     for cp in stores:
         cp.wait()
 
-    def sent(d, _):
-        for f in range(F):
-            c_copy(f, d, dev).wait_send()
-        return 0
-
-    lax.fori_loop(1, G, sent, 0)
-
     def handed(d, _):
         for f in range(F):
             w_copy(f, d, dev).wait_send()
+            q_copy(f, d).wait_send()
+            c_copy(f, d).wait_send()
             slot = lax.rem(dev + G - 2 * d, G)
             p_copy(f, d, wg.at[f, slot], slot).wait_send()
         return 0
@@ -350,6 +372,7 @@
     lax.fori_loop(1, half_group, handed, 0)
     for f in range(F):
         p_copy(f, 0, fac.at[f], dev).wait_send()
+        q_copy(f, 0).wait_send()
     for k in range(8):
         for h in range(H):
             for d in range(1, M):
@@ -399,8 +422,10 @@
             pltpu.SemaphoreType.DMA((F, G // 2)),
             pltpu.SemaphoreType.DMA((F, G // 2)),
             pltpu.SemaphoreType.DMA((F, G // 2)),
-            pltpu.SemaphoreType.DMA((F, G)),
-            pltpu.SemaphoreType.DMA((F, G)),
+            pltpu.SemaphoreType.DMA((F, G // 2)),
+            pltpu.SemaphoreType.DMA((F, G // 2)),
+            pltpu.SemaphoreType.DMA((F, G // 2)),
+            pltpu.SemaphoreType.DMA((F, G // 2)),
         ],
         compiler_params=pltpu.CompilerParams(
             collective_id=0, has_side_effects=True, vmem_limit_bytes=60 * 1024 * 1024

time: 116 us -> 109 us (0.940)
  Pallas kernels: 109 us -> 101 us
    pallas_call x1, Pallas kernels: 109 us -> 101 us  [step(): pl.pallas_call(functools.partial(kernel, G, M), out_shape=(jax.ShapeDtype...]
where the time goes in v3:
time: 109 us; the launch traced here: 107 us
  Pallas kernels  101 us (93%)
  local copies, waits for them, and re-layouts  5.51 us (5%)
    pallas_call x1, Pallas kernels, step(): pl.pallas_call(functools.partial(kernel, G, M), out_shape=(jax.ShapeDtype...  101 us
    unnamed x10, local copies, waits for them, and re-layouts  5.51 us

profile of v3, /device:TPU:25, one launch (start us, length us, event | category | flops | bytes accessed | tf_op | source)
XLA Modules:
  0.0 107.2 jit_solution(10952652310385541265)
XLA Ops:
  0.6 101.0 %shard_map.84 = (bf16[2048,256]{1,0:T(8,128)(2,1)}, bf16[2048,256]{1,0:T(8,128)(2,1)}, f32[4,16,2048]{2,1,0:T(8,128)}, bf16[1,4,16,16384]{3,2,1,0:T(8,128)(2,1)}) custom-call(bf16[2048,256]{1,0:T(8,128)(2,1)} %inp.1, bf16[2048,256]{1,0:T(8,128)(2,1)} %cot.1, bf16[4,16,2048]{2,1,0:T(8,128)(2,1)} %fac.1, s32[4,16]{1,0:T(4,128)} %expo.1, ...), custom_call_target="tpu_custom_call" | custom-call | tf_op jit(solution)/shard_map/pallas_call | solution.py:389
  101.6 0.0 copy-start.1
  101.6 0.0 copy-start.2
  101.6 0.0 copy-start
  101.7 2.4 %copy.13 = bf16[2048,256]{1,0:T(8,128)(2,1)} copy(bf16[2048,256]{1,0:T(8,128)(2,1)} %get-tuple-element.8) | data formatting | bytes 2097152
  104.1 0.0 copy-done.1
  104.1 1.0 copy.14
  105.0 0.0 copy-done.2
  105.0 0.8 copy.15
  105.8 0.0 copy-done
  105.8 1.3 %copy.16 = bf16[1,4,16,16384]{3,2,1,0:T(8,128)(2,1)} copy(bf16[1,4,16,16384]{3,2,1,0:T(8,128)(2,1)S(1)} %copy-done) | data formatting | bytes 4194304
Async XLA Ops:
  101.6 2.4 %copy-start.1 = (bf16[2048,256]{1,0:T(8,128)(2,1)S(1)}, bf16[2048,256]{1,0:T(8,128)(2,1)}, u32[]{:S(2)}) copy-start(bf16[2048,256]{1,0:T(8,128)(2,1)} %get-tuple-element.9) | copy-start | bytes 3145732
  101.6 3.4 %copy-start.2 = (f32[4,16,2048]{2,1,0:T(8,128)S(1)}, f32[4,16,2048]{2,1,0:T(8,128)}, u32[]{:S(2)}) copy-start(f32[4,16,2048]{2,1,0:T(8,128)} %get-tuple-element.10) | copy-start | bytes 1572868
  101.6 4.2 %copy-start = (bf16[1,4,16,16384]{3,2,1,0:T(8,128)(2,1)S(1)}, bf16[1,4,16,16384]{3,2,1,0:T(8,128)(2,1)}, u32[]{:S(2)}) copy-start(bf16[1,4,16,16384]{3,2,1,0:T(8,128)(2,1)} %get-tuple-element.11) | copy-start | bytes 6291460
